TPU v7x, 128 devices: a whole 4x4x4 slice. The times are simulated.
128 devices in a mesh: ctx: 32 (over x, y, core), row: 4 (over z).
Axes of the slice: x: 4, y: 4, z: 4, core: 2. Of those that a mesh axis runs over, the one named last changes fastest.
Arguments:
- latent_cache: bfloat16 [131072, 576], P(('ctx', 'row')), may hold values from -8 to 8
- index_keys: bfloat16 [131072, 128], P('ctx'), may hold values from -6 to 6
- query_latent: bfloat16 [512, 128, 576], P(('row', 'ctx')), may hold values from -100 to 99
- index_query: bfloat16 [512, 64, 128], P(('row', 'ctx')), may hold values from -0.5 to 0.5
- index_gates: bfloat16 [512, 64], P(('row', 'ctx')), may hold values from -0.75 to 0.75
- selected: int32 [512, 2048], P(('row', 'ctx')), may hold values from 0 to 131071, as said below
Outputs:
- attended: bfloat16 [512, 128, 512], P(('row', 'ctx'))
- index_scores: float32 [512, 131072], P('row', 'ctx')
Inputs may be any that keep to these rules, and one draw needn't show every extreme that they name: `selected`: each row names 2048 different tokens. Among the tokens of one index of ctx (s * 4096 <= t < (s + 1) * 4096) a row names at most 256, and exactly 256 in one such range; a row names at most one token in each aligned run of 16 tokens.
All inputs are finite; a program needn't handle non-finite values.
Results may differ from a plain program's by a relative error of at most 0.0045.
Values may be sent and summed in bfloat16 or wider, within the bound.
A program may use at most 256 MiB of HBM per device.

v0:
```python
import jax
import jax.numpy as jnp
from jax import lax
from jax.sharding import PartitionSpec as P

LATENT = 512
SCORE_DIM = 192
SEL_MOST = 256
TOK_DEV = 4096


def index_block(iquery, gates, index_keys):
    count = iquery.shape[0]
    groups = count // 8
    heads = iquery.shape[1]
    query_blocks = iquery.reshape(groups, 8 * heads, iquery.shape[2])
    gate_blocks = gates.astype(jnp.float32).reshape(groups, 8, heads)

    def one_block(pair):
        block, gate = pair
        logits = jnp.einsum("qd,td->qt", block, index_keys, preferred_element_type=jnp.float32)
        logits = logits.reshape(8, heads, logits.shape[1])
        return jnp.sum(gate[:, :, None] * jnp.maximum(logits, 0.0), axis=1)

    result = lax.map(one_block, (query_blocks, gate_blocks))
    return result.reshape(count, result.shape[2])


def slot_table(place, value, slots):

    def one_row(pair):
        where_to, what = pair
        hit = where_to[:, None] == jnp.arange(slots, dtype=jnp.int32)[None, :]
        return jnp.max(jnp.where(hit, what[:, None], -1), axis=0)

    return lax.map(one_row, (place, value))


def pick_rows(source, table, spacing):
    blocks = source.reshape(source.shape[0] // spacing, spacing, source.shape[1])
    offset = table % spacing
    onehot = (
        (offset[:, :, None] == jnp.arange(spacing, dtype=jnp.int32)[None, None, :])
        & (table >= 0)[:, :, None]
    ).astype(jnp.bfloat16)
    rows_out = jnp.einsum("gsj,sjd->gsd", onehot, blocks, preferred_element_type=jnp.float32)
    return rows_out.astype(jnp.bfloat16)


def weigh(queries, keys, valid):
    scores = jnp.einsum(
        "ghd,gsd->ghs", queries, keys, preferred_element_type=jnp.float32
    ) * SCORE_DIM ** (-0.5)
    return jnp.where(valid[:, None, :], scores, -1e30)


def combine(masked, peak, keys, valid):
    weights = jnp.where(valid[:, None, :], jnp.exp(masked - peak[:, :, None]), 0.0).astype(
        jnp.bfloat16
    )
    totals = jnp.sum(weights.astype(jnp.float32), axis=2)
    sums = jnp.einsum(
        "ghs,gsd->ghd", weights, keys[:, :, :LATENT], preferred_element_type=jnp.float32
    )
    return (sums, totals)


def body(latent_cache, index_keys, query_latent, index_query, index_gates, selected):
    spacing = TOK_DEV // SEL_MOST
    slab = lax.all_gather(latent_cache, "row", axis=0, tiled=True)
    queries, iquery, gates = (
        lax.all_gather(query_latent, "ctx", axis=0, tiled=True),
        lax.all_gather(index_query, "ctx", axis=0, tiled=True),
        lax.all_gather(index_gates, "ctx", axis=0, tiled=True),
    )
    picks = lax.all_gather(selected, "ctx", axis=0, tiled=True)
    index_scores = index_block(iquery, gates, index_keys)
    local = picks - lax.axis_index("ctx") * TOK_DEV
    mine = (local >= 0) & (local < TOK_DEV)
    place = jnp.where(mine, local // spacing, SEL_MOST)
    table = slot_table(place, local, SEL_MOST)
    valid = table >= 0
    keys = pick_rows(slab, table, spacing)
    masked = weigh(queries, keys, valid)
    peak = lax.pmax(jnp.max(masked, axis=2), "ctx")
    sums, totals = combine(masked, peak, keys, valid)
    summed, total = (
        lax.psum_scatter(sums, "ctx", scatter_dimension=0, tiled=True),
        lax.psum_scatter(totals, "ctx", scatter_dimension=0, tiled=True),
    )
    attended = (summed / total[:, :, None]).astype(jnp.bfloat16)
    return (attended, index_scores)


def solution(mesh):
    return jax.shard_map(
        body,
        mesh=mesh,
        in_specs=(
            P(("ctx", "row"), None),
            P("ctx", None),
            P(("row", "ctx"), None, None),
            P(("row", "ctx"), None, None),
            P(("row", "ctx"), None),
            P(("row", "ctx"), None),
        ),
        out_specs=(P(("row", "ctx"), None, None), P("row", "ctx")),
        check_vma=False,
    )
```

profile of v0, /device:TPU:1, one launch (start us, length us, event | category | flops | bytes accessed | tf_op | source)
XLA Modules:
  0.0 751.0 jit_solution(6434805967596199768)
XLA Ops:
  9.4 46.8 %all-gather.13.cloned.1.call-done = s32[32,4,2048]{2,1,0:T(4,128)} async-done(((s32[1,4,2048]{2,1,0:T(4,128)}), s32[32,4,2048]{2,1,0:T(4,128)}) %all-gather.13.cloned.1.call-update) | async-done | bytes 1048592 | tf_op jit(solution)/shard_map/all_gather | solution.py:76
  56.2 1.3 broadcast_subtract_fusion
  58.6 166.7 %while.22 = (s32[]{:T(128)}, s32[128,256]{1,0:T(8,128)S(1)}, s32[128,2048]{1,0:T(8,128)S(1)}, s32[128,2048]{1,0:T(8,128)S(1)}) while((s32[]{:T(128)}, s32[128,256]{1,0:T(8,128)S(1)}, s32[128,2048]{1,0:T(8,128)S(1)}, s32[128,2048]{1,0:T(8,128)S(1)}) %tuple.46), condition=%wide.region_2.3_spmd.clone, body=%wide.region_0.2_spmd.sunk.clone | while | flops 1572610 | bytes 52293 | solution.py:36
  58.7 1.2 select_reduce_fusion.3
  60.0 1.2 select_reduce_fusion.3
  61.3 1.2 select_reduce_fusion.3
  62.6 1.2 select_reduce_fusion.3
  63.9 1.2 select_reduce_fusion.3
  65.2 1.2 select_reduce_fusion.3
  66.5 1.2 select_reduce_fusion.3
  67.8 1.2 select_reduce_fusion.3
  69.1 1.2 select_reduce_fusion.3
  70.4 1.2 select_reduce_fusion.3
  71.7 1.2 select_reduce_fusion.3
  73.0 1.2 select_reduce_fusion.3
  74.3 1.2 select_reduce_fusion.3
  75.6 1.2 select_reduce_fusion.3
  76.9 1.2 select_reduce_fusion.3
  78.2 1.2 select_reduce_fusion.3
  79.5 1.2 select_reduce_fusion.3
  80.8 1.2 select_reduce_fusion.3
  82.1 1.2 select_reduce_fusion.3
  83.4 1.2 select_reduce_fusion.3
  84.7 1.2 select_reduce_fusion.3
  86.0 1.2 select_reduce_fusion.3
  87.3 1.2 select_reduce_fusion.3
  88.6 1.2 select_reduce_fusion.3
  90.0 1.2 select_reduce_fusion.3
  91.3 1.2 select_reduce_fusion.3
  92.6 1.2 select_reduce_fusion.3
  93.9 1.2 select_reduce_fusion.3
  95.2 1.2 select_reduce_fusion.3
  96.5 1.2 select_reduce_fusion.3
  97.8 1.2 select_reduce_fusion.3
  225.7 7.6 %copy.22 = bf16[4096,576]{1,0:T(8,128)(2,1)} copy(bf16[4096,576]{0,1:T(8,128)(2,1)} %all-gather.7.cloned.1.call-done) | data formatting | bytes 9437184 | tf_op jit(solution)/shard_map/all_gather | solution.py:70
  233.4 18.0 %convert_bitcast_fusion = bf16[128,256,576]{0,2,1:T(8,128)(2,1)} fusion(bf16[256,16,576]{2,1,0:T(8,128)(2,1)} %bitcast.69, s32[128,256]{0,1:T(8,128)S(1)} %copy.20, pred[128,256]{0,1:T(8,128)(4,1)S(1)} %copy.21), kind=kOutput, calls=%fused_computation.9 | convolution fusion | flops 623902720 | bytes 42631168 | tf_op jit(solution)/shard_map/gsj,sjd->gsd/dot_general | solution.py:46
  251.4 51.8 %copy.23 = bf16[128,256,576]{1,2,0:T(8,128)(2,1)} copy(bf16[128,256,576]{0,2,1:T(8,128)(2,1)} %convert_bitcast_fusion) | data formatting | bytes 75497472 | tf_op jit(solution)/shard_map/convert_element_type | solution.py:47
  303.2 30.3 %bitcast_reduce_fusion = (f32[128,128]{1,0:T(8,128)}, f32[128,256,128]{2,1,0:T(8,128)}) fusion(pred[128,256]{1,0:T(8,128)(4,1)S(1)} %broadcast_compare_fusion, bf16[128,256,576]{1,2,0:T(8,128)(2,1)} %copy.23, bf16[128,128,576]{1,2,0:T(8,128)(2,1)} %all-gather.9.cloned.1.call-done), kind=kOutput, calls=%fused_computation.11 | convolution fusion | flops 4844404736 | bytes 73498624 | tf_op jit(solution)/shard_map/ghd,gsd->ghs/dot_general | solution.py:51
  334.2 23.0 %slice.4 = bf16[128,256,512]{0,2,1:T(8,128)(2,1)} slice(bf16[128,256,576]{0,2,1:T(8,128)(2,1)} %convert_bitcast_fusion), slice={[0:128], [0:256], [0:512]} | slice | bytes 67108864 | tf_op jit(solution)/shard_map/slice | solution.py:63
  357.2 44.9 %copy.25 = bf16[128,256,512]{2,1,0:T(8,128)(2,1)} copy(bf16[128,256,512]{0,2,1:T(8,128)(2,1)} %slice.4) | data formatting | bytes 67108864 | tf_op jit(solution)/shard_map/slice | solution.py:63
  402.0 28.0 %all-reduce.4.cloned.1.call-done = f32[128,128]{1,0:T(8,128)} async-done(((f32[128,128]{1,0:T(8,128)}), f32[128,128]{1,0:T(8,128)}) %all-reduce.4.cloned.1.call-update) | async-done | bytes 65552 | tf_op jit(solution)/shard_map/pmax | solution.py:85
  430.0 14.2 %convert_reduce_fusion = f32[128,128]{1,0:T(8,128)} fusion(f32[128,128]{1,0:T(8,128)} %all-reduce.4.cloned.1.call-done, f32[128,256,128]{2,1,0:T(8,128)} %get-tuple-element.74, pred[128,256]{1,0:T(8,128)(4,1)S(1)} %broadcast_compare_fusion), kind=kLoop, calls=%fused_computation.15 | loop fusion | flops 29343744 | bytes 16941056 | tf_op jit(solution)/shard_map/reduce_sum | solution.py:61
  444.5 32.7 %fusion.12 = f32[128,128,512]{2,1,0:T(8,128)} fusion(bf16[128,256,512]{2,1,0:T(8,128)(2,1)} %copy.25, f32[128,256,128]{2,1,0:T(8,128)} %get-tuple-element.74, f32[128,128]{1,0:T(8,128)S(1)} %copy-done, pred[128,256]{1,0:T(8,128)(4,1)S(1)} %broadcast_compare_fusion), kind=kOutput, calls=%fused_computation.38 | convolution fusion | flops 4315938816 | bytes 83984384 | tf_op jit(solution)/shard_map/ghs,gsd->ghd/dot_general | solution.py:62
  479.1 23.1 %all-gather.1 = bf16[32,4,64]{2,1,0:T(4,128)(2,1)S(1)} all-gather(bf16[1,4,64]{2,1,0:T(4,128)(2,1)S(1)} %bitcast.79), channel_id=1, replica_groups=mesh['ctx'=32,'row'=4] {'ctx'}, dimensions={0}, use_global_device_ids=true | all-gather | bytes 16896 | tf_op jit(solution)/shard_map/all_gather | solution.py:74
  502.2 46.3 %while.23 = (s32[]{:T(128)}, f32[16,8,4096]{2,1,0:T(8,128)}, f32[16,8,64]{2,1,0:T(8,128)S(1)}, bf16[16,512,128]{2,1,0:T(8,128)(2,1)}, bf16[4096,128]{1,0:T(8,128)(2,1)S(1)}) while((s32[]{:T(128)}, f32[16,8,4096]{2,1,0:T(8,128)}, f32[16,8,64]{2,1,0:T(8,128)S(1)}, bf16[16,512,128]{2,1,0:T(8,128)(2,1)}, ...), condition=%wide.region_10.11_spmd.clone, body=%wide.region_8.10_spmd.sunk.clone | while | flops 543129600 | bytes 1841233 | solution.py:25
  503.2 1.3 multiply_reduce_fusion.3
  506.1 1.3 multiply_reduce_fusion.3
  509.0 1.3 multiply_reduce_fusion.3
  511.9 1.3 multiply_reduce_fusion.3
  514.8 1.3 multiply_reduce_fusion.3
  517.7 1.3 multiply_reduce_fusion.3
  520.6 1.3 multiply_reduce_fusion.3
  523.4 1.3 multiply_reduce_fusion.3
  526.3 1.3 multiply_reduce_fusion.3
  529.2 1.3 multiply_reduce_fusion.3
  532.1 1.3 multiply_reduce_fusion.3
  535.0 1.3 multiply_reduce_fusion.3
  537.9 1.3 multiply_reduce_fusion.3
  540.8 1.3 multiply_reduce_fusion.3
  543.7 1.3 multiply_reduce_fusion.3
  546.6 1.3 multiply_reduce_fusion.3
  548.6 26.0 %all-reduce.6.cloned.1.call-done = f32[128,128]{1,0:T(8,128)} async-done(((f32[128,128]{1,0:T(8,128)}), f32[128,128]{1,0:T(8,128)}) %all-reduce.6.cloned.1.call-update) | async-done | bytes 65552
  575.2 166.7 %reduce-scatter.2.cloned.1.call-done = f32[4,128,512]{2,1,0:T(8,128)} async-done(((f32[128,128,512]{2,1,0:T(8,128)}), f32[4,128,512]{2,1,0:T(8,128)}) %reduce-scatter.2.cloned.1.call-update) | async-done | bytes 1048592 | tf_op jit(solution)/shard_map/reduce_scatter | solution.py:88
  742.0 2.2 divide_convert_fusion
  (437 shorter events, 157.2 us)
Async XLA Ops:
  7.2 49.1 %all-gather.13.cloned.1.call-start = ((), (), s32[]{:S(2)}) async-start(), calls=%async_computation.6 | async-start | bytes 1081344 | tf_op jit(solution)/shard_map/all_gather | solution.py:76
  7.9 217.8 %all-gather.7.cloned.1.call-start = ((), (), s32[]{:S(2)}) async-start(), calls=%async_computation.1 | async-start | bytes 5898240 | tf_op jit(solution)/shard_map/all_gather | solution.py:70
  8.6 294.6 %all-gather.9.cloned.1.call-start = ((), (), s32[]{:S(2)}) async-start(), calls=%async_computation.2 | async-start | bytes 19464192 | tf_op jit(solution)/shard_map/all_gather | solution.py:72
  9.4 420.6 %all-reduce.4.cloned.1.call-start = ((), (), s32[]{:S(2)}) async-start(), calls=%async_computation.3 | async-start | bytes 131072 | tf_op jit(solution)/shard_map/pmax | solution.py:85
  333.5 168.7 %all-gather.11.cloned.1.call-start = ((), (), s32[]{:S(2)}) async-start(), calls=%async_computation.5 | async-start | bytes 2162688 | tf_op jit(solution)/shard_map/all_gather | solution.py:73
  334.1 240.4 %all-reduce.6.cloned.1.call-start = ((), (), s32[]{:S(2)}) async-start(), calls=%async_computation.7 | async-start | bytes 131072
  430.0 14.5 %copy-start = (f32[128,128]{1,0:T(8,128)S(1)}, f32[128,128]{1,0:T(8,128)}, u32[]{:S(2)}) copy-start(f32[128,128]{1,0:T(8,128)} %all-reduce.4.cloned.1.call-done) | copy-start | bytes 196612
  444.3 297.7 %reduce-scatter.2.cloned.1.call-start = ((), (), s32[]{:S(2)}) async-start(), calls=%async_computation.4 | async-start | bytes 34603008 | tf_op jit(solution)/shard_map/reduce_scatter | solution.py:88
  477.2 0.7 copy-start.3
  477.2 1.9 copy-start.1
  477.2 25.1 %copy-start.2 = (bf16[4096,128]{1,0:T(8,128)(2,1)S(1)}, bf16[4096,128]{1,0:T(8,128)(2,1)}, u32[]{:S(2)}) copy-start(bf16[4096,128]{1,0:T(8,128)(2,1)} %param.11) | copy-start | bytes 3145732
Sparse Core Ops, SparseCore 0:
  10.2 45.9 all-gather.12
  57.9 51.6 all-gather.6
  111.9 78.0 all-gather.8
  333.7 96.3 all-reduce.3
  432.1 42.4 all-gather.10
  478.3 96.2 all-reduce.5
  578.4 163.4 reduce-scatter.1
where the time goes:
time: 754 us; the launch traced here: 751 us
  waiting for transfers between devices  270 us (36%)
  other arithmetic  173 us (23%)
  local copies, waits for them, and re-layouts  163 us (22%)
  matrix products  101 us (13%)
  blocking collectives  23.1 us (3%)
  between operations  14.9 us (2%)
    reduce_scatter x1, waiting for transfers between devices, body(): lax.psum_scatter(sums, 'ctx', scatter_dimension=0, tiled=True)  167 us
    reduce_max x128, other arithmetic, one_row(): return jnp.max(jnp.where(hit, what[:, None], -1), axis=0)  155 us
    slice x2, local copies, waits for them, and re-layouts, combine(): keys[:, :, :LATENT]  67.9 us
    convert_element_type x1, local copies, waits for them, and re-layouts, pick_rows(): return rows_out.astype(jnp.bfloat16)  51.8 us
    all_gather x1, waiting for transfers between devices, body(): picks = lax.all_gather(selected, 'ctx', axis=0, tiled=True)  46.8 us
    dot_general x1, matrix products, combine(): jnp.einsum('ghs,gsd->ghd', weights, keys[:, :, :LATENT], preferred_elemen...  32.7 us
    dot_general x1, matrix products, weigh(): jnp.einsum('ghd,gsd->ghs', queries, keys, preferred_element_type=jnp.floa...  30.3 us
    unnamed x8, waiting for transfers between devices  28.6 us
  transfers between devices with their start and end apart: 7, of which 4 were waited for; matrix products, arithmetic and copies ran while one was open for 54% of the time, Pallas kernels for 0%

commit v1 on v0

--- a/solution.py
+++ b/solution.py
@@ -73,7 +73,8 @@
         lax.all_gather(index_query, "ctx", axis=0, tiled=True),
         lax.all_gather(index_gates, "ctx", axis=0, tiled=True),
     )
-    picks = lax.all_gather(selected, "ctx", axis=0, tiled=True)
+    sent = jnp.stack([selected] * lax.axis_size("ctx"))
+    picks = jnp.concatenate(lax.all_to_all(sent, "ctx", 0, 0), axis=0)
     index_scores = index_block(iquery, gates, index_keys)
     local = picks - lax.axis_index("ctx") * TOK_DEV
     mine = (local >= 0) & (local < TOK_DEV)

time: 754 us -> 731 us (0.969)
  waiting for transfers between devices: 270 us -> 240 us
  starting transfers between devices: 0.45 us -> 9 us
    all_gather x1 -> x0, waiting for transfers between devices: 46.8 us -> none  [body(): picks = lax.all_gather(selected, 'ctx', axis=0, tiled=True)]
    all_to_all x0 -> x1, waiting for transfers between devices: none -> 16.1 us  [body(): picks = jnp.concatenate(lax.all_to_all(sent, 'ctx', 0, 0), axis=0)]
    all_to_all x0 -> x1, starting transfers between devices: none -> 8.58 us  [body(): picks = jnp.concatenate(lax.all_to_all(sent, 'ctx', 0, 0), axis=0)]
    unnamed x8 -> x7, waiting for transfers between devices: 28.6 us -> 27.9 us
  transfers between devices with their start and end apart: 7 -> 7, of which waited for: 4 -> 4; matrix products, arithmetic and copies ran while one was open for 54% -> 55% of each run, Pallas kernels for 0% -> 0%
where the time goes in v1:
time: 731 us; the launch traced here: 728 us
  waiting for transfers between devices  240 us (33%)
  other arithmetic  172 us (24%)
  local copies, waits for them, and re-layouts  163 us (22%)
  matrix products  101 us (14%)
  blocking collectives  23.1 us (3%)
  between operations  15 us (2%)
  starting transfers between devices  9 us (1%)
    reduce_scatter x1, waiting for transfers between devices, body(): lax.psum_scatter(sums, 'ctx', scatter_dimension=0, tiled=True)  166 us
    reduce_max x128, other arithmetic, one_row(): return jnp.max(jnp.where(hit, what[:, None], -1), axis=0)  155 us
    slice x2, local copies, waits for them, and re-layouts, combine(): keys[:, :, :LATENT]  65.6 us
    convert_element_type x1, local copies, waits for them, and re-layouts, pick_rows(): return rows_out.astype(jnp.bfloat16)  52 us
    dot_general x1, matrix products, combine(): jnp.einsum('ghs,gsd->ghd', weights, keys[:, :, :LATENT], preferred_elemen...  32.7 us
    dot_general x1, matrix products, weigh(): jnp.einsum('ghd,gsd->ghs', queries, keys, preferred_element_type=jnp.floa...  30.3 us
    pmax x1, waiting for transfers between devices, body(): peak = lax.pmax(jnp.max(masked, axis=2), 'ctx')  29.6 us
    unnamed x7, waiting for transfers between devices  27.9 us
  transfers between devices with their start and end apart: 7, of which 4 were waited for; matrix products, arithmetic and copies ran while one was open for 55% of the time, Pallas kernels for 0%

profile of v1, /device:TPU:1, one launch (start us, length us, event | category | flops | bytes accessed | tf_op | source)
XLA Modules:
  0.0 728.2 jit_solution(13690168536128693705)
XLA Ops:
  7.9 2.0 stack.2
  9.9 8.6 %all-to-all-start = ((s32[32,4,2048]{2,1,0:T(4,128)}), s32[32,4,2048]{2,1,0:T(4,128)S(1)}, u32[]{:S(2)}, u32[]{:S(2)}) async-start(s32[32,4,2048]{2,1,0:T(4,128)} %stack.2), calls=%async_computation | async-start | bytes 2097152 | tf_op jit(solution)/shard_map/all_to_all | solution.py:77
  19.3 16.1 %all-to-all-done = s32[32,4,2048]{2,1,0:T(4,128)S(1)} async-done(((s32[32,4,2048]{2,1,0:T(4,128)}), s32[32,4,2048]{2,1,0:T(4,128)S(1)}, u32[]{:S(2)}, u32[]{:S(2)}) %all-to-all-start) | async-done | bytes 1048608 | tf_op jit(solution)/shard_map/all_to_all | solution.py:77
  36.5 166.7 %while.22 = (s32[]{:T(128)}, s32[128,256]{1,0:T(8,128)S(1)}, s32[128,2048]{1,0:T(8,128)S(1)}, s32[128,2048]{1,0:T(8,128)S(1)}) while((s32[]{:T(128)}, s32[128,256]{1,0:T(8,128)S(1)}, s32[128,2048]{1,0:T(8,128)S(1)}, s32[128,2048]{1,0:T(8,128)S(1)}) %tuple.46), condition=%wide.region_2.3_spmd.clone, body=%wide.region_0.2_spmd.sunk.clone | while | flops 1572610 | bytes 52293 | solution.py:36
  36.6 1.2 select_reduce_fusion.3
  37.9 1.2 select_reduce_fusion.3
  39.2 1.2 select_reduce_fusion.3
  40.5 1.2 select_reduce_fusion.3
  41.8 1.2 select_reduce_fusion.3
  43.1 1.2 select_reduce_fusion.3
  44.4 1.2 select_reduce_fusion.3
  45.7 1.2 select_reduce_fusion.3
  47.0 1.2 select_reduce_fusion.3
  48.3 1.2 select_reduce_fusion.3
  49.6 1.2 select_reduce_fusion.3
  50.9 1.2 select_reduce_fusion.3
  52.2 1.2 select_reduce_fusion.3
  53.5 1.2 select_reduce_fusion.3
  54.8 1.2 select_reduce_fusion.3
  56.1 1.2 select_reduce_fusion.3
  57.4 1.2 select_reduce_fusion.3
  58.7 1.2 select_reduce_fusion.3
  60.0 1.2 select_reduce_fusion.3
  61.3 1.2 select_reduce_fusion.3
  62.6 1.2 select_reduce_fusion.3
  63.9 1.2 select_reduce_fusion.3
  65.2 1.2 select_reduce_fusion.3
  66.5 1.2 select_reduce_fusion.3
  67.8 1.2 select_reduce_fusion.3
  69.1 1.2 select_reduce_fusion.3
  70.5 1.2 select_reduce_fusion.3
  71.8 1.2 select_reduce_fusion.3
  73.1 1.2 select_reduce_fusion.3
  74.4 1.2 select_reduce_fusion.3
  203.6 7.7 %copy.22 = bf16[4096,576]{1,0:T(8,128)(2,1)} copy(bf16[4096,576]{0,1:T(8,128)(2,1)} %all-gather.5.cloned.1.call-done) | data formatting | bytes 9437184 | tf_op jit(solution)/shard_map/all_gather | solution.py:70
  211.3 18.0 %convert_bitcast_fusion = bf16[128,256,576]{0,2,1:T(8,128)(2,1)} fusion(bf16[256,16,576]{2,1,0:T(8,128)(2,1)} %bitcast.68, s32[128,256]{0,1:T(8,128)S(1)} %copy.20, pred[128,256]{0,1:T(8,128)(4,1)S(1)} %copy.21), kind=kOutput, calls=%fused_computation.9 | convolution fusion | flops 623902720 | bytes 42631168 | tf_op jit(solution)/shard_map/gsj,sjd->gsd/dot_general | solution.py:46
  229.3 52.0 %copy.23 = bf16[128,256,576]{1,2,0:T(8,128)(2,1)} copy(bf16[128,256,576]{0,2,1:T(8,128)(2,1)} %convert_bitcast_fusion) | data formatting | bytes 75497472 | tf_op jit(solution)/shard_map/convert_element_type | solution.py:47
  281.2 30.3 %bitcast_reduce_fusion = (f32[128,128]{1,0:T(8,128)}, f32[128,256,128]{2,1,0:T(8,128)}) fusion(pred[128,256]{1,0:T(8,128)(4,1)S(1)} %broadcast_compare_fusion, bf16[128,256,576]{1,2,0:T(8,128)(2,1)} %copy.23, bf16[128,128,576]{1,2,0:T(8,128)(2,1)} %all-gather.7.cloned.1.call-done), kind=kOutput, calls=%fused_computation.11 | convolution fusion | flops 4844404736 | bytes 73498624 | tf_op jit(solution)/shard_map/ghd,gsd->ghs/dot_general | solution.py:51
  312.4 23.0 %slice.4 = bf16[128,256,512]{0,2,1:T(8,128)(2,1)} slice(bf16[128,256,576]{0,2,1:T(8,128)(2,1)} %convert_bitcast_fusion), slice={[0:128], [0:256], [0:512]} | slice | bytes 67108864 | tf_op jit(solution)/shard_map/slice | solution.py:63
  335.3 42.6 %copy.25 = bf16[128,256,512]{2,1,0:T(8,128)(2,1)} copy(bf16[128,256,512]{0,2,1:T(8,128)(2,1)} %slice.4) | data formatting | bytes 67108864 | tf_op jit(solution)/shard_map/slice | solution.py:63
  377.9 29.6 %all-reduce.4.cloned.1.call-done = f32[128,128]{1,0:T(8,128)} async-done(((f32[128,128]{1,0:T(8,128)}), f32[128,128]{1,0:T(8,128)}) %all-reduce.4.cloned.1.call-update) | async-done | bytes 65552 | tf_op jit(solution)/shard_map/pmax | solution.py:86
  407.6 14.2 %convert_reduce_fusion = f32[128,128]{1,0:T(8,128)} fusion(f32[128,128]{1,0:T(8,128)} %all-reduce.4.cloned.1.call-done, f32[128,256,128]{2,1,0:T(8,128)} %get-tuple-element.74, pred[128,256]{1,0:T(8,128)(4,1)S(1)} %broadcast_compare_fusion), kind=kLoop, calls=%fused_computation.15 | loop fusion | flops 29343744 | bytes 16941056 | tf_op jit(solution)/shard_map/reduce_sum | solution.py:61
  421.9 32.7 %fusion.12 = f32[128,128,512]{2,1,0:T(8,128)} fusion(bf16[128,256,512]{2,1,0:T(8,128)(2,1)} %copy.25, f32[128,256,128]{2,1,0:T(8,128)} %get-tuple-element.74, f32[128,128]{1,0:T(8,128)S(1)} %copy-done, pred[128,256]{1,0:T(8,128)(4,1)S(1)} %broadcast_compare_fusion), kind=kOutput, calls=%fused_computation.38 | convolution fusion | flops 4315938816 | bytes 83984384 | tf_op jit(solution)/shard_map/ghs,gsd->ghd/dot_general | solution.py:62
  456.5 23.1 %all-gather = bf16[32,4,64]{2,1,0:T(4,128)(2,1)S(1)} all-gather(bf16[1,4,64]{2,1,0:T(4,128)(2,1)S(1)} %bitcast.77), channel_id=1, replica_groups=mesh['ctx'=32,'row'=4] {'ctx'}, dimensions={0}, use_global_device_ids=true | all-gather | bytes 16896 | tf_op jit(solution)/shard_map/all_gather | solution.py:74
  479.7 46.3 %while.23 = (s32[]{:T(128)}, f32[16,8,4096]{2,1,0:T(8,128)}, f32[16,8,64]{2,1,0:T(8,128)S(1)}, bf16[16,512,128]{2,1,0:T(8,128)(2,1)}, bf16[4096,128]{1,0:T(8,128)(2,1)S(1)}) while((s32[]{:T(128)}, f32[16,8,4096]{2,1,0:T(8,128)}, f32[16,8,64]{2,1,0:T(8,128)S(1)}, bf16[16,512,128]{2,1,0:T(8,128)(2,1)}, ...), condition=%wide.region_10.11_spmd.clone, body=%wide.region_8.10_spmd.sunk.clone | while | flops 543129600 | bytes 1841233 | solution.py:25
  480.7 1.3 multiply_reduce_fusion.3
  483.6 1.3 multiply_reduce_fusion.3
  486.5 1.3 multiply_reduce_fusion.3
  489.4 1.3 multiply_reduce_fusion.3
  492.3 1.3 multiply_reduce_fusion.3
  495.2 1.3 multiply_reduce_fusion.3
  498.0 1.3 multiply_reduce_fusion.3
  500.9 1.3 multiply_reduce_fusion.3
  503.8 1.3 multiply_reduce_fusion.3
  506.7 1.3 multiply_reduce_fusion.3
  509.6 1.3 multiply_reduce_fusion.3
  512.5 1.3 multiply_reduce_fusion.3
  515.4 1.3 multiply_reduce_fusion.3
  518.3 1.3 multiply_reduce_fusion.3
  521.2 1.3 multiply_reduce_fusion.3
  524.1 1.3 multiply_reduce_fusion.3
  526.1 26.0 %all-reduce.6.cloned.1.call-done = f32[128,128]{1,0:T(8,128)} async-done(((f32[128,128]{1,0:T(8,128)}), f32[128,128]{1,0:T(8,128)}) %all-reduce.6.cloned.1.call-update) | async-done | bytes 65552
  552.7 166.5 %reduce-scatter.2.cloned.1.call-done = f32[4,128,512]{2,1,0:T(8,128)} async-done(((f32[128,128,512]{2,1,0:T(8,128)}), f32[4,128,512]{2,1,0:T(8,128)}) %reduce-scatter.2.cloned.1.call-update) | async-done | bytes 1048592 | tf_op jit(solution)/shard_map/reduce_scatter | solution.py:89
  719.2 2.2 divide_convert_fusion
  (437 shorter events, 157.8 us)
Async XLA Ops:
  7.2 196.5 %all-gather.5.cloned.1.call-start = ((), (), s32[]{:S(2)}) async-start(), calls=%async_computation.2 | async-start | bytes 5898240 | tf_op jit(solution)/shard_map/all_gather | solution.py:70
  9.9 25.5 %all-to-all-start = ((s32[32,4,2048]{2,1,0:T(4,128)}), s32[32,4,2048]{2,1,0:T(4,128)S(1)}, u32[]{:S(2)}, u32[]{:S(2)}) async-start(s32[32,4,2048]{2,1,0:T(4,128)} %stack.2), calls=%async_computation | async-start | bytes 2097152 | tf_op jit(solution)/shard_map/all_to_all | solution.py:77
  18.4 262.8 %all-gather.7.cloned.1.call-start = ((), (), s32[]{:S(2)}) async-start(), calls=%async_computation.3 | async-start | bytes 19464192 | tf_op jit(solution)/shard_map/all_gather | solution.py:72
  19.2 388.3 %all-reduce.4.cloned.1.call-start = ((), (), s32[]{:S(2)}) async-start(), calls=%async_computation.4 | async-start | bytes 131072 | tf_op jit(solution)/shard_map/pmax | solution.py:86
  311.5 168.2 %all-gather.9.cloned.1.call-start = ((), (), s32[]{:S(2)}) async-start(), calls=%async_computation.6 | async-start | bytes 2162688 | tf_op jit(solution)/shard_map/all_gather | solution.py:73
  312.1 239.9 %all-reduce.6.cloned.1.call-start = ((), (), s32[]{:S(2)}) async-start(), calls=%async_computation.7 | async-start | bytes 131072
  407.5 14.3 %copy-start = (f32[128,128]{1,0:T(8,128)S(1)}, f32[128,128]{1,0:T(8,128)}, u32[]{:S(2)}) copy-start(f32[128,128]{1,0:T(8,128)} %all-reduce.4.cloned.1.call-done) | copy-start | bytes 196612
  421.8 297.4 %reduce-scatter.2.cloned.1.call-start = ((), (), s32[]{:S(2)}) async-start(), calls=%async_computation.5 | async-start | bytes 34603008 | tf_op jit(solution)/shard_map/reduce_scatter | solution.py:89
  454.5 0.7 copy-start.3
  454.5 2.0 copy-start.1
  454.5 25.2 %copy-start.2 = (bf16[4096,128]{1,0:T(8,128)(2,1)S(1)}, bf16[4096,128]{1,0:T(8,128)(2,1)}, u32[]{:S(2)}) copy-start(bf16[4096,128]{1,0:T(8,128)(2,1)} %param.11) | copy-start | bytes 3145732
Sparse Core Ops, SparseCore 0:
  9.6 55.8 all-gather.4
  67.7 78.0 all-gather.6
  311.7 95.8 all-reduce.3
  409.7 42.4 all-gather.8
  455.8 96.1 all-reduce.5
  555.8 163.3 reduce-scatter.1
